TPU v7x, 128 devices: a whole 4x4x4 slice. The times are simulated.
128 devices in a mesh: dp: 8 (over z, y_hi), head: 16 (over y_lo, x, core).
Axes of the slice: x: 4, y: 4 (y_hi: 2, y_lo: 2; y = y_hi * 2 + y_lo), z: 4, core: 2. Of those that a mesh axis runs over, the one named last changes fastest.
Arguments:
- ckpt_query: bfloat16 [4, 8192, 8192], P(None, ('dp', 'head')), may hold values from -0.125 to 0.125
- ckpt_key: bfloat16 [4, 8192, 1024], P(None, ('dp', 'head')), may hold values from -0.125 to 0.125
- ckpt_value: bfloat16 [4, 8192, 1024], P(None, ('dp', 'head')), may hold values from -0.125 to 0.125
- ckpt_output: bfloat16 [4, 8192, 8192], P(None, ('head', 'dp')), may hold values from -0.125 to 0.125
- hidden_in: bfloat16 [4096, 8192], P('dp'), may hold values from -17 to 17
- segment_ids: int32 [8, 512], P('dp'), may hold values from 0 to 3, never falling along the last dimension, each value on 1 to 256 neighbouring positions
Outputs:
- attn_out: bfloat16 [4096, 8192], P('dp', 'head')
All inputs are finite; a program needn't handle non-finite values.
Results may differ from a plain program's by a relative error of at most 0.01.
The roundings to bfloat16 on the way count: a program that leaves them out, or rounds other values in their place, can miss the bound.
Values may be sent and summed in bfloat16 or wider, within the bound.
A program may use at most 128 MiB of HBM per device.

v0:
```python
import jax
import jax.numpy as jnp
from jax import lax
from jax.sharding import PartitionSpec as P

rope_base = 500000.0


def average(stack):
    return (jnp.sum(stack.astype(jnp.float32), axis=0) * 0.25).astype(jnp.bfloat16)


def rotate(values, positions):
    half = values.shape[-1] // 2
    freq = rope_base ** (-2.0 * jnp.arange(half, dtype=jnp.float32) / values.shape[-1])
    angle = positions[:, None] * freq[None, :]
    cosine = jnp.cos(angle)[:, None, :]
    sine = jnp.sin(angle)[:, None, :]
    first = values[..., :half]
    second = values[..., half:]
    return jnp.concatenate(
        [first * cosine - second * sine, second * cosine + first * sine], axis=-1
    )


def shards(ckpt_query, ckpt_key, ckpt_value, ckpt_output, hidden_in, segment_ids):
    n_dp = lax.axis_size("dp")
    n_head = lax.axis_size("head")
    rows, wide = ckpt_query.shape[1:]
    kv_wide = ckpt_key.shape[2]
    output_rows = lax.all_gather(average(ckpt_output), "dp", axis=0, tiled=True)
    mean_query = average(ckpt_query).reshape(rows, n_head, wide // n_head)
    mean_key = average(ckpt_key).reshape(rows, n_head, kv_wide // n_head)
    mean_value = average(ckpt_value).reshape(rows, n_head, kv_wide // n_head)
    packed = jnp.concatenate([mean_query, mean_key, mean_value], axis=2).transpose(1, 0, 2)
    moved = lax.all_to_all(packed, "head", split_axis=0, concat_axis=0, tiled=True)
    gathered = lax.all_gather(moved.reshape(n_head * rows, -1), "dp", axis=0, tiled=True)
    tok = hidden_in.shape[0]
    projected = jnp.dot(hidden_in, gathered, preferred_element_type=jnp.float32)
    query = projected[:, : wide // n_head]
    head_size = 2 * kv_wide // n_head
    own = projected[:, wide // n_head :]
    position = lax.axis_index("head")
    other = lax.ppermute(own, "head", [(i, i ^ 1) for i in range(n_head)])
    half = head_size // 2
    lower = position % 2 == 0
    low = jnp.where(lower, own, other)
    high = jnp.where(lower, other, own)
    keys = jnp.concatenate([low[:, :half], high[:, :half]], axis=1)
    values = jnp.concatenate([low[:, half:], high[:, half:]], axis=1)
    heads_here = query.shape[1] // head_size
    positions = jnp.arange(tok, dtype=jnp.float32)
    q_rot = rotate(query.reshape(tok, heads_here, head_size), positions).astype(jnp.bfloat16)
    k_rot = rotate(keys.reshape(tok, 1, head_size), positions)[:, 0].astype(jnp.bfloat16)
    v_b = values.astype(jnp.bfloat16)
    scores = jnp.einsum(
        "qhd,kd->hqk", q_rot, k_rot, preferred_element_type=jnp.float32
    ) * head_size ** (-0.5)
    order = jnp.arange(tok, dtype=jnp.int32)
    segment = segment_ids[0]
    allowed = (order[:, None] >= order[None, :]) & (segment[:, None] == segment[None, :])
    scores = jnp.where(allowed[None], scores, -1e30)
    peak = jnp.max(scores, axis=-1, keepdims=True)
    weights = jnp.exp(scores - peak)
    probs = (weights / jnp.sum(weights, axis=-1, keepdims=True)).astype(jnp.bfloat16)
    context = jnp.einsum("hqk,kd->qhd", probs, v_b, preferred_element_type=jnp.float32)
    context = context.astype(jnp.bfloat16).reshape(tok, heads_here * head_size)
    everyone = lax.all_gather(context, "head", axis=0)
    weight = output_rows.reshape(output_rows.shape[0], n_head, wide // n_head)
    result = lax.dot_general(
        everyone, weight, (((0, 2), (1, 2)), ((), ())), preferred_element_type=jnp.float32
    )
    return result.astype(jnp.bfloat16)


def solution(mesh):
    placed = (
        P(None, ("dp", "head"), None),
        P(None, ("dp", "head"), None),
        P(None, ("dp", "head"), None),
        P(None, ("head", "dp"), None),
        P("dp", None),
        P("dp", None),
    )
    return jax.shard_map(
        shards, mesh=mesh, in_specs=placed, out_specs=P("dp", "head"), check_vma=False
    )
```

profile of v0, /device:TPU:1, one launch (start us, length us, event | category | flops | bytes accessed | tf_op | source)
XLA Modules:
  0.0 342.0 jit_solution(17139786216191566086)
XLA Ops:
  6.5 1.1 convert_reduce_fusion.3
  7.9 1.2 convert_reduce_fusion.2
  9.3 3.2 convert_reduce_fusion.1
  12.6 0.4 copy.40
  13.4 25.1 %all_to_all.5 = bf16[16,64,640]{2,1,0:T(8,128)(2,1)} all-to-all(bf16[16,64,640]{2,1,0:T(8,128)(2,1)S(1)} %copy.26), channel_id=1, replica_groups=mesh['dp'=8,'head'=16] {'head'}, dimensions={0} | all-to-all | bytes 2621440 | tf_op jit(solution)/shard_map/all_to_all | solution.py:36
  38.6 3.2 convert_reduce_fusion
  41.8 1.2 multiply_convert_fusion
  43.3 1.0 fusion.14
  44.3 120.4 %all-gather.4.cloned.1.call-done = bf16[8192,640]{1,0:T(8,128)(2,1)} async-done(((bf16[1024,640]{1,0:T(8,128)(2,1)}), bf16[8192,640]{1,0:T(8,128)(2,1)}) %all-gather.4.cloned.1.call-update) | async-done | bytes 10485776 | tf_op jit(solution)/shard_map/all_gather | solution.py:37
  164.6 11.2 %convolution_bitcast_fusion = f32[512,640]{0,1:T(8,128)S(1)} fusion(bf16[8192,640]{1,0:T(8,128)(2,1)} %all-gather.4.cloned.1.call-done, bf16[512,8192]{1,0:T(8,128)(2,1)} %param.10), kind=kOutput, calls=%fused_computation.13 | convolution fusion | flops 5368709120 | bytes 20185088 | tf_op jit(solution)/shard_map/dot_general | solution.py:39
  175.9 0.8 slice.42
  176.8 1.3 collective-permute-start
  178.6 0.3 copy.38
  179.2 0.4 collective-permute-done
  179.6 1.1 broadcast_select_fusion.1
  180.8 0.6 subtract_convert_fusion.1
  181.4 0.8 fusion.9
  182.1 2.1 fusion.26
  184.3 0.5 fusion.6
  184.8 1.0 copy.31
  185.8 86.2 %all-gather.8.cloned.1.call-done = bf16[512,8192]{1,0:T(8,128)(2,1)} async-done(((bf16[64,8192]{1,0:T(8,128)(2,1)}), bf16[512,8192]{1,0:T(8,128)(2,1)}) %all-gather.8.cloned.1.call-update) | async-done | bytes 8388624 | tf_op jit(solution)/shard_map/all_gather | solution.py:31
  272.0 12.0 %copy.32 = bf16[512,8192]{0,1:T(8,128)(2,1)} copy(bf16[512,8192]{1,0:T(8,128)(2,1)} %all-gather.8.cloned.1.call-done) | data formatting | bytes 16777216 | tf_op jit(solution)/shard_map/all_gather | solution.py:31
  284.1 40.3 %all-gather.6.cloned.1.call-done = bf16[16,512,512]{2,1,0:T(8,128)(2,1)} async-done(((bf16[1,512,512]{2,1,0:T(8,128)(2,1)}), bf16[16,512,512]{2,1,0:T(8,128)(2,1)}) %all-gather.6.cloned.1.call-update) | async-done | bytes 8388624 | tf_op jit(solution)/shard_map/all_gather | solution.py:68
  324.4 11.0 %fusion.7 = bf16[512,512]{1,0:T(8,128)(2,1)} fusion(bf16[16,512,512]{2,1,0:T(8,128)(2,1)} %all-gather.6.cloned.1.call-done, bf16[512,16,512]{0,2,1:T(8,128)(2,1)} %bitcast.42), kind=kOutput, calls=%fused_computation.17 | convolution fusion | flops 4295229440 | bytes 17301504 | tf_op jit(solution)/shard_map/dot_general | solution.py:70
  (28 shorter events, 2.2 us)
Async XLA Ops:
  6.5 158.1 %all-gather.4.cloned.1.call-start = ((), (), s32[]{:S(2)}) async-start(), calls=%async_computation.1 | async-start | bytes 11796480 | tf_op jit(solution)/shard_map/all_gather | solution.py:37
  38.6 4.5 %copy-start.1 = (s32[1,512]{1,0:T(1,128)S(1)}, s32[1,512]{1,0:T(1,128)}, u32[]{:S(2)}) copy-start(s32[1,512]{1,0:T(1,128)} %param.11) | copy-start | bytes 6148
  38.6 233.4 %all-gather.8.cloned.1.call-start = ((), (), s32[]{:S(2)}) async-start(), calls=%async_computation.3 | async-start | bytes 9437184 | tf_op jit(solution)/shard_map/all_gather | solution.py:31
  43.0 281.4 %all-gather.6.cloned.1.call-start = ((), (), s32[]{:S(2)}) async-start(), calls=%async_computation.2 | async-start | bytes 8912896 | tf_op jit(solution)/shard_map/all_gather | solution.py:68
  175.9 2.3 copy-start
  176.8 2.8 collective-permute-start
Sparse Core Ops, SparseCore 0:
  38.7 125.9 all-gather.3
  167.0 104.9 all-gather.7
  273.7 50.6 all-gather.5
where the time goes:
time: 343 us; the launch traced here: 342 us
  waiting for transfers between devices  247 us (72%)
  blocking collectives  25.1 us (7%)
  matrix products  23.5 us (7%)
  local copies, waits for them, and re-layouts  15.7 us (5%)
  other arithmetic  15.4 us (4%)
  between operations  13.3 us (4%)
    all_gather x1, waiting for transfers between devices, shards(): lax.all_gather(moved.reshape(n_head * rows, -1), 'dp', axis=0, tiled=True)  120 us
    all_gather x1, waiting for transfers between devices, shards(): output_rows = lax.all_gather(average(ckpt_output), 'dp', axis=0, tiled=True)  86.2 us
    all_gather x1, waiting for transfers between devices, shards(): everyone = lax.all_gather(context, 'head', axis=0)  40.3 us
    all_to_all x1, blocking collectives, shards(): lax.all_to_all(packed, 'head', split_axis=0, concat_axis=0, tiled=True)  25.1 us
    all_gather x1, local copies, waits for them, and re-layouts, shards(): output_rows = lax.all_gather(average(ckpt_output), 'dp', axis=0, tiled=True)  12 us
    dot_general x1, matrix products, shards(): projected = jnp.dot(hidden_in, gathered, preferred_element_type=jnp.float32)  11.2 us
    dot_general x1, matrix products, shards(): lax.dot_general(everyone, weight, (((0, 2), (1, 2)), ((), ())), preferred...  11 us
    reduce_sum x4, other arithmetic, average(): jnp.sum(stack.astype(jnp.float32), axis=0) * 0.25  8.62 us
  transfers between devices with their start and end apart: 4, of which 4 were waited for; matrix products, arithmetic and copies ran while one was open for 11% of the time, Pallas kernels for 0%

commit v1 on v0

--- a/solution.py
+++ b/solution.py
@@ -28,7 +28,11 @@
     n_head = lax.axis_size("head")
     rows, wide = ckpt_query.shape[1:]
     kv_wide = ckpt_key.shape[2]
-    output_rows = lax.all_gather(average(ckpt_output), "dp", axis=0, tiled=True)
+    x = average(ckpt_output)
+    n_dev = lax.axis_size("dp")
+    blocks = jnp.stack([x for _ in range(n_dev)])
+    blocks = lax.all_to_all(blocks, "dp", split_axis=0, concat_axis=0)
+    output_rows = jnp.concatenate(blocks, axis=0)
     mean_query = average(ckpt_query).reshape(rows, n_head, wide // n_head)
     mean_key = average(ckpt_key).reshape(rows, n_head, kv_wide // n_head)
     mean_value = average(ckpt_value).reshape(rows, n_head, kv_wide // n_head)

time: 343 us -> 362 us (1.055)
  blocking collectives: 25.1 us -> 163 us
  waiting for transfers between devices: 247 us -> 125 us
  matrix products: 23.5 us -> 28.8 us
    all_to_all x0 -> x1, blocking collectives: none -> 137 us  [shards(): blocks = lax.all_to_all(blocks, 'dp', split_axis=0, concat_axis=0)]
    all_gather x1 -> x0, waiting for transfers between devices: 86.2 us -> none  [shards(): output_rows = lax.all_gather(average(ckpt_output), 'dp', axis=0, tiled=True)]
    all_gather x1, waiting for transfers between devices: 40.3 us -> 0.01 us  [shards(): everyone = lax.all_gather(context, 'head', axis=0)]
    all_gather x1 -> x0, local copies, waits for them, and re-layouts: 12 us -> none  [shards(): output_rows = lax.all_gather(average(ckpt_output), 'dp', axis=0, tiled=True)]
    unnamed x7 -> x8, local copies, waits for them, and re-layouts: 1.03 us -> 12 us
    dot_general x1, matrix products: 11 us -> 16.3 us  [shards(): lax.dot_general(everyone, weight, (((0, 2), (1, 2)), ((), ())), preferred...]
    all_gather x1, waiting for transfers between devices: 120 us -> 125 us  [shards(): lax.all_gather(moved.reshape(n_head * rows, -1), 'dp', axis=0, tiled=True)]
  transfers between devices with their start and end apart: 4 -> 3, of which waited for: 4 -> 2; matrix products, arithmetic and copies ran while one was open for 11% -> 5% of each run, Pallas kernels for 0% -> 0%
where the time goes in v1:
time: 362 us
  blocking collectives  163 us (45%)
  waiting for transfers between devices  125 us (35%)
  matrix products  28.8 us (8%)
  local copies, waits for them, and re-layouts  15.7 us (4%)
  other arithmetic  14.4 us (4%)
  between operations  13.7 us (4%)
    all_to_all x1, blocking collectives, shards(): blocks = lax.all_to_all(blocks, 'dp', split_axis=0, concat_axis=0)  137 us
    all_gather x1, waiting for transfers between devices, shards(): lax.all_gather(moved.reshape(n_head * rows, -1), 'dp', axis=0, tiled=True)  125 us
    all_to_all x1, blocking collectives, shards(): lax.all_to_all(packed, 'head', split_axis=0, concat_axis=0, tiled=True)  25.1 us
    dot_general x1, matrix products, shards(): lax.dot_general(everyone, weight, (((0, 2), (1, 2)), ((), ())), preferred...  16.3 us
    unnamed x8, local copies, waits for them, and re-layouts  12 us
    dot_general x1, matrix products, shards(): projected = jnp.dot(hidden_in, gathered, preferred_element_type=jnp.float32)  11.2 us
    reduce_sum x4, other arithmetic, average(): jnp.sum(stack.astype(jnp.float32), axis=0) * 0.25  8.62 us
  transfers between devices with their start and end apart: 3, of which 2 were waited for; matrix products, arithmetic and copies ran while one was open for 5% of the time, Pallas kernels for 0%

profile of v1, /device:TPU:1, one launch (start us, length us, event | category | flops | bytes accessed | tf_op | source)
XLA Modules:
  0.0 361.7 jit_solution(1842490860181930722)
XLA Ops:
  6.5 1.1 convert_reduce_fusion.3
  7.9 1.2 convert_reduce_fusion.2
  9.3 3.2 convert_reduce_fusion.1
  12.6 0.4 copy.37
  13.4 25.1 %all_to_all.10 = bf16[16,64,640]{2,1,0:T(8,128)(2,1)} all-to-all(bf16[16,64,640]{2,1,0:T(8,128)(2,1)S(1)} %copy.25), channel_id=1, replica_groups=mesh['dp'=8,'head'=16] {'head'}, dimensions={0} | all-to-all | bytes 2621440 | tf_op jit(solution)/shard_map/all_to_all | solution.py:40
  38.9 1.0 fusion.21
  39.9 124.8 %all-gather.3.cloned.1.call-done = bf16[8192,640]{1,0:T(8,128)(2,1)} async-done(((bf16[1024,640]{1,0:T(8,128)(2,1)}), bf16[8192,640]{1,0:T(8,128)(2,1)}) %all-gather.3.cloned.1.call-update) | async-done | bytes 10485776 | tf_op jit(solution)/shard_map/all_gather | solution.py:41
  164.7 11.2 %convolution_bitcast_fusion = f32[512,640]{0,1:T(8,128)S(1)} fusion(bf16[8192,640]{1,0:T(8,128)(2,1)} %all-gather.3.cloned.1.call-done, bf16[512,8192]{1,0:T(8,128)(2,1)} %param.10), kind=kOutput, calls=%fused_computation.15 | convolution fusion | flops 5368709120 | bytes 20185088 | tf_op jit(solution)/shard_map/dot_general | solution.py:43
  175.9 0.8 slice.42
  176.7 1.3 collective-permute-start
  178.2 0.3 copy.36
  178.5 0.3 copy.35
  179.2 0.4 collective-permute-done
  179.6 1.1 broadcast_select_fusion.1
  180.8 0.6 subtract_convert_fusion.1
  181.3 0.8 fusion.16
  182.1 2.1 fusion.33
  184.3 0.5 fusion.14
  184.8 1.0 copy.30
  185.8 3.2 convert_reduce_fusion
  189.1 1.1 stack.2
  190.2 137.4 %all_to_all.11 = bf16[8,64,8192]{2,1,0:T(8,128)(2,1)} all-to-all(bf16[8,64,8192]{2,1,0:T(8,128)(2,1)S(1)} %stack.2), channel_id=1, replica_groups=mesh['dp'=8,'head'=16] {'dp'}, dimensions={0} | all-to-all | bytes 16777216 | tf_op jit(solution)/shard_map/all_to_all | solution.py:34
  327.6 11.0 %copy.38 = bf16[64,8,16,512]{3,2,1,0:T(8,128)(2,1)} copy(bf16[64,8,16,512]{3,1,2,0:T(8,128)(2,1)} %bitcast.43) | data formatting | bytes 16777216
  338.6 16.3 %fusion.11 = bf16[512,512]{1,0:T(8,128)(2,1)} fusion(bf16[16,512,512]{2,1,0:T(8,128)(2,1)} %all-gather.5.cloned.1.call-done, bf16[512,16,512]{2,1,0:T(8,128)(2,1)} %bitcast.44), kind=kOutput, calls=%fused_computation.18 | convolution fusion | flops 4295229440 | bytes 17301504 | tf_op jit(solution)/shard_map/dot_general | solution.py:74
  (27 shorter events, 1.9 us)
Async XLA Ops:
  6.5 158.1 %all-gather.3.cloned.1.call-start = ((), (), s32[]{:S(2)}) async-start(), calls=%async_computation.2 | async-start | bytes 11796480 | tf_op jit(solution)/shard_map/all_gather | solution.py:41
  12.9 25.8 %copy-start.1 = (s32[1,512]{1,0:T(1,128)S(1)}, s32[1,512]{1,0:T(1,128)}, u32[]{:S(2)}) copy-start(s32[1,512]{1,0:T(1,128)} %param.11) | copy-start | bytes 6148
  38.6 300.0 %all-gather.5.cloned.1.call-start = ((), (), s32[]{:S(2)}) async-start(), calls=%async_computation.3 | async-start | bytes 8912896 | tf_op jit(solution)/shard_map/all_gather | solution.py:72
  175.9 2.3 copy-start
  176.7 2.8 collective-permute-start
Sparse Core Ops, SparseCore 0:
  38.7 125.9 all-gather.2
  185.9 89.0 all-gather.4
